TPU v7x, 32 devices: a whole 2x2x4 slice. The times are simulated.
32 devices in a mesh: dp: 4 (over y, x), shard: 8 (over z, core).
Axes of the slice: x: 2, y: 2, z: 4, core: 2. Of those that a mesh axis runs over, the one named last changes fastest.
Arguments:
- id_table: float32 [262144, 128], P(('dp', 'shard')), may hold values from -6 to 6
- ada_state: float32 [262144], P(('dp', 'shard')), may hold values from 0.01 to 1
- user_first: float32 [128, 512], replicated, may hold values from -0.5 to 0.5
- user_second: float32 [512, 128], replicated, may hold values from -0.25 to 0.25
- item_first: float32 [128, 512], replicated, may hold values from -0.5 to 0.5
- item_second: float32 [512, 128], replicated, may hold values from -0.25 to 0.25
- fetch_rows: int32 [32, 4, 8, 72], P(('dp', 'shard')), may hold values from 0 to 8191
- lookup_slots: int32 [32, 1536], P(('dp', 'shard')), may hold values from 0 to 2303
Outputs:
- new_table: float32 [262144, 128], P(('dp', 'shard'))
- new_state: float32 [262144], P(('dp', 'shard'))
- user_first_grad: float32 [128, 512], replicated
- user_second_grad: float32 [512, 128], replicated
- item_first_grad: float32 [128, 512], replicated
- item_second_grad: float32 [512, 128], replicated
- mean_loss: float32 [], replicated
All inputs are finite; a program needn't handle non-finite values.
Results may differ from a plain program's by a relative error of at most 0.0038.
The roundings to bfloat16 on the way count: a program that leaves them out, or rounds other values in their place, can miss the bound.
Values may be sent and summed in bfloat16 or wider, within the bound.
No kernel may reach another device: no remote copies, remote signals or barrier semaphores. Data moves between devices by JAX's collectives and lax.ppermute only.
A program may use at most 128 MiB of HBM per device.

v0:
```python
import jax
import jax.numpy as jnp
from jax import lax
from jax.sharding import PartitionSpec as P

EXAMPLES_ON_CHIP = 512
highest = lax.Precision.HIGHEST
logit_divisor = 0.025
learn_rate = 0.1
epsilon = 1e-08


def tower_pass(looked, first_w, second_w):
    hidden_act = jax.nn.silu(
        jnp.dot(looked, first_w, precision=highest, preferred_element_type=jnp.float32)
    )
    tower_out = jnp.dot(hidden_act, second_w, precision=highest, preferred_element_type=jnp.float32)
    return tower_out / jnp.sqrt(jnp.sum(tower_out * tower_out, axis=1, keepdims=True) + 1e-06)


def score_block(user_half_precision, candidate_half_precision):
    return (
        jnp.dot(user_half_precision, candidate_half_precision.T, preferred_element_type=jnp.float32)
        / logit_divisor
    )


def cand_step(candidate_half_precision, user_half_precision):
    exponent = jnp.exp(score_block(user_half_precision, candidate_half_precision))
    collected_entries = jnp.dot(
        exponent.astype(jnp.bfloat16), candidate_half_precision, preferred_element_type=jnp.float32
    )
    return (jnp.sum(exponent, axis=1), collected_entries)


def item_term(user_half_precision, log_z, candidate_half_precision):
    softmax = jnp.exp(
        score_block(user_half_precision, candidate_half_precision) - log_z[:, None]
    ).astype(jnp.bfloat16)
    return jnp.dot(softmax.T, user_half_precision, preferred_element_type=jnp.float32)


def per_device(
    id_table, ada_state, user_first, user_second, item_first, item_second, fetch_rows, lookup_slots
):
    target_index_vector = id_table.shape[1]
    examples_on_chip = EXAMPLES_ON_CHIP
    asked_rows = lax.all_to_all(
        lax.all_to_all(fetch_rows[0], "dp", split_axis=0, concat_axis=0, tiled=True),
        "shard",
        split_axis=1,
        concat_axis=1,
        tiled=True,
    )
    fetched = jnp.take(id_table, asked_rows.reshape(-1), axis=0).reshape(
        asked_rows.shape + (target_index_vector,)
    )
    returned = lax.all_to_all(
        lax.all_to_all(fetched, "dp", split_axis=0, concat_axis=0, tiled=True),
        "shard",
        split_axis=1,
        concat_axis=1,
        tiled=True,
    )
    slot_rows = returned.reshape(-1, target_index_vector)
    slot_index = lookup_slots[0]
    looked = jnp.take(slot_rows, slot_index, axis=0)
    user_vec, user_pull = jax.vjp(tower_pass, looked[:examples_on_chip], user_first, user_second)
    item_vec, item_pull = jax.vjp(tower_pass, looked[examples_on_chip:], item_first, item_second)
    user_half_precision = user_vec.astype(jnp.bfloat16)
    item_bf = item_vec.astype(jnp.bfloat16)
    query_single_float = user_half_precision.astype(jnp.float32)
    resident_target_entries = item_bf[:examples_on_chip].astype(jnp.float32)
    matching_pair_logit = (
        jnp.sum(query_single_float * resident_target_entries, axis=1) / logit_divisor
    )
    reduced_aggregates, collected_entries = cand_step(
        lax.all_gather(item_bf, "dp", axis=0, tiled=True), user_half_precision
    )
    log_z = jnp.log(reduced_aggregates)
    target_derivative_accrual = item_term(
        lax.all_gather(user_vec, "dp", axis=0, tiled=True).astype(jnp.bfloat16),
        lax.all_gather(log_z, "dp", axis=0, tiled=True),
        item_bf,
    )
    query_adjoint = (
        collected_entries / reduced_aggregates[:, None] - resident_target_entries
    ) / logit_divisor
    target_adjoint = (
        target_derivative_accrual.at[:examples_on_chip].add(-query_single_float) / logit_divisor
    )
    user_look, user_first_g, user_second_g = user_pull(query_adjoint)
    item_look, item_first_g, item_second_g = item_pull(target_adjoint)
    look_grads = jnp.concatenate([user_look, item_look], axis=0)
    slot_grads = jnp.zeros_like(slot_rows).at[slot_index].add(look_grads)
    sent_back = lax.all_to_all(
        lax.all_to_all(
            slot_grads.reshape(returned.shape).astype(jnp.bfloat16),
            "dp",
            split_axis=0,
            concat_axis=0,
            tiled=True,
        ),
        "shard",
        split_axis=1,
        concat_axis=1,
        tiled=True,
    ).astype(jnp.float32)
    grad_rows = (
        jnp.zeros_like(id_table)
        .at[asked_rows.reshape(-1)]
        .add(sent_back.reshape(-1, target_index_vector))
    )
    new_state = ada_state + jnp.mean(grad_rows * grad_rows, axis=1)
    new_table = id_table - learn_rate * grad_rows / (jnp.sqrt(new_state)[:, None] + epsilon)
    loss_part = jnp.sum(log_z - matching_pair_logit)
    summed = lax.psum(
        (user_first_g, user_second_g, item_first_g, item_second_g, loss_part), ("dp", "shard")
    )
    shard_number = lax.axis_size("dp") * lax.axis_size("shard")
    return (
        new_table,
        new_state,
        summed[0] / shard_number,
        summed[1] / shard_number,
        summed[2] / shard_number,
        summed[3] / shard_number,
        summed[4] / (shard_number * examples_on_chip),
    )


def solution(mesh):
    return jax.shard_map(
        per_device,
        mesh=mesh,
        in_specs=(
            P(("dp", "shard"), None),
            P(("dp", "shard")),
            P(),
            P(),
            P(),
            P(),
            P(("dp", "shard"), None, None, None),
            P(("dp", "shard"), None),
        ),
        out_specs=(P(("dp", "shard"), None), P(("dp", "shard")), P(), P(), P(), P(), P()),
        check_vma=False,
    )
```

profile of v0, /device:TPU:0, one launch (start us, length us, event | category | flops | bytes accessed | tf_op | source)
XLA Modules:
  0.0 361.9 jit_solution(15782953325688524731)
XLA Ops:
  7.2 10.0 %all_to_all.30 = s32[4,8,72]{2,1,0:T(8,128)S(1)} all-to-all(s32[4,8,72]{2,1,0:T(8,128)} %bitcast.34), channel_id=1, replica_groups=mesh['dp'=4,'shard'=8] {'dp'}, dimensions={0} | all-to-all | bytes 18432 | tf_op jit(solution)/shard_map/all_to_all | solution.py:49
  17.2 10.3 %all_to_all.31 = s32[4,8,72]{2,0,1:T(4,128)S(1)} all-to-all(s32[4,8,72]{2,0,1:T(4,128)S(1)} %copy.24), channel_id=1, replica_groups=mesh['dp'=4,'shard'=8] {'shard'}, dimensions={1} | all-to-all | bytes 18432 | tf_op jit(solution)/shard_map/all_to_all | solution.py:48
  28.3 6.1 %gather_fusion = f32[2304,128]{1,0:T(8,128)S(1)} fusion(f32[8192,128]{1,0:T(8,128)} %param.10, s32[3072]{0:T(1024)S(1)} %pad_clamp_fusion), kind=kCustom, calls=%fused_computation | custom fusion | bytes 2368512 | tf_op jit(solution)/shard_map/jit(_take)/gather | solution.py:55
  34.9 18.2 %all_to_all.32 = f32[4,8,72,128]{3,2,1,0:T(8,128)S(1)} all-to-all(f32[4,8,72,128]{3,2,1,0:T(8,128)S(1)} %broadcast_select_fusion), channel_id=1, replica_groups=mesh['dp'=4,'shard'=8] {'dp'}, dimensions={0} | all-to-all | bytes 2359296 | tf_op jit(solution)/shard_map/all_to_all | solution.py:59
  54.2 3.6 all-to-all-start.3
  57.9 29.1 %all-to-all-done.3 = f32[4,8,72,128]{3,2,0,1:T(8,128)S(1)} async-done(((f32[4,8,72,128]{3,2,0,1:T(8,128)}), f32[4,8,72,128]{3,2,0,1:T(8,128)S(1)}, u32[]{:S(2)}, u32[]{:S(2)}) %all-to-all-start.3) | async-done | bytes 1179680 | tf_op jit(solution)/shard_map/all_to_all | solution.py:58
  91.9 2.7 multiply_reduce_fusion.2
  97.3 2.7 multiply_reduce_fusion.4
  101.3 11.5 %all_gather.10 = bf16[2048,128]{0,1:T(8,128)(2,1)} all-gather(bf16[512,128]{0,1:T(8,128)(2,1)S(1)} %get-tuple-element.24), channel_id=1, replica_groups=mesh['dp'=4,'shard'=8] {'dp'}, dimensions={0}, use_global_device_ids=true | all-gather | bytes 655360 | tf_op jit(solution)/shard_map/all_gather | solution.py:82
  112.8 8.4 %all-gather.3.cloned.1.call-done = bf16[4096,128]{0,1:T(8,128)(2,1)} async-done(((bf16[1024,128]{0,1:T(8,128)(2,1)}), bf16[4096,128]{0,1:T(8,128)(2,1)}) %all-gather.3.cloned.1.call-update) | async-done | bytes 1048592 | tf_op jit(solution)/shard_map/all_gather | solution.py:78
  121.2 5.8 %fusion = (f32[512]{0:T(512)S(1)}, f32[512,4096]{1,0:T(8,128)}) fusion(bf16[512,128]{0,1:T(8,128)(2,1)S(1)} %get-tuple-element.24, bf16[4096,128]{0,1:T(8,128)(2,1)} %all-gather.3.cloned.1.call-done), kind=kOutput, calls=%fused_computation.6 | convolution fusion | flops 541064704 | bytes 9570304 | tf_op jit(solution)/shard_map/dot_general | solution.py:23
  127.6 8.8 %all-gather = f32[4,1,512]{2,1,0:T(1,128)} all-gather(f32[1,1,512]{2,1,0:T(1,128)S(1)} %bitcast.36), channel_id=1, replica_groups=mesh['dp'=4,'shard'=8] {'dp'}, dimensions={0}, use_global_device_ids=true | all-gather | bytes 10240 | tf_op jit(solution)/shard_map/all_gather | solution.py:83
  136.5 4.1 %fusion.10 = f32[1024,128]{0,1:T(8,128)} fusion(bf16[1024,128]{0,1:T(8,128)(2,1)S(1)} %copy-done.3, f32[2048]{0:T(1024)} %bitcast.35, bf16[2048,128]{0,1:T(8,128)(2,1)} %all_gather.10), kind=kOutput, calls=%fused_computation.19 | convolution fusion | flops 1080033280 | bytes 1318912 | tf_op jit(solution)/shard_map/dot_general | solution.py:40
  144.6 3.8 %fusion.6 = f32[1024,512]{1,0:T(8,128)S(1)} fusion(f32[1024,512]{1,0:T(8,128)S(1)} %fusion.30, f32[512,128]{1,0:T(8,128)S(1)} %copy-done, f32[1024,128]{0,1:T(8,128)} %copy-done.5, f32[1024,128]{0,1:T(8,128)} %fusion.37, f32[1024]{0:T(1024)S(1)} %multiply_multiply_fusion, f32[1024]{0:T(1024)} %copy-done.17), kind=kOutput, calls=%fused_computation.14 | convolution fusion | flops 810680320 | bytes 5513216 | tf_op jit(solution)/shard_map/transpose(jvp())/dot_general | solution.py:17
  154.8 2.6 fusion.43
  160.0 9.3 %scatter_custom_fusion = f32[2304,128]{1,0:T(8,128)S(1)} fusion(s32[1536]{0:T(1024)S(1)} %fusion.48, f32[1024,128]{1,0:T(8,128)} %fusion.58, f32[]{:T(128)} %constant.111, f32[512,128]{1,0:T(8,128)S(1)} %fusion.57, f32[]{:T(128)} %constant.90.clone.1), kind=kCustom, calls=%fused_computation.28 | custom fusion | flops 393216 | bytes 1966088 | tf_op jit(solution)/shard_map/scatter-add | solution.py:95
  170.2 3.5 all-to-all-start.4
  173.7 6.2 %fusion.32 = f32[512,128]{1,0:T(8,128)} fusion(f32[1024,512]{1,0:T(8,128)} %copy-done.4, f32[1024,128]{0,1:T(8,128)} %copy-done.5, f32[1024,128]{0,1:T(8,128)} %fusion.37, f32[1024]{0:T(1024)S(1)} %copy-done.26, f32[1024]{0:T(1024)S(1)} %copy-done.18), kind=kOutput, calls=%fused_computation.45 | convolution fusion | flops 808058880 | bytes 3416064 | tf_op jit(solution)/shard_map/transpose(jvp())/dot_general | solution.py:17
  181.5 4.6 %all-to-all-start.5 = ((bf16[4,8,72,128]{3,2,0,1:T(8,128)(2,1)}), bf16[4,8,72,128]{3,2,0,1:T(8,128)(2,1)S(1)}, u32[]{:S(2)}, u32[]{:S(2)}) async-start(bf16[4,8,72,128]{3,2,0,1:T(8,128)(2,1)} %copy.29), calls=%async_computation.5 | async-start | bytes 1179648 | tf_op jit(solution)/shard_map/all_to_all | solution.py:96
  187.7 40.8 %psum.39 = f32[]{:T(128)} all-reduce(f32[]{:T(128)} %get-tuple-element.29), channel_id=1, replica_groups=mesh['dp'=4,'shard'=8] {'dp','shard'}, use_global_device_ids=true, to_apply=%region_14.15 | all-reduce | flops 1 | bytes 8 | tf_op jit(solution)/shard_map/psum | solution.py:117
  229.1 96.8 %all-reduce.3.cloned.1.call-done = (f32[128,512]{1,0:T(8,128)}, f32[512,128]{1,0:T(8,128)}, f32[128,512]{1,0:T(8,128)}, f32[512,128]{1,0:T(8,128)}) async-done(((f32[128,512]{1,0:T(8,128)}, f32[512,128]{1,0:T(8,128)}, f32[128,512]{1,0:T(8,128)}, f32[512,128]{1,0:T(8,128)}), (f32[128,512]{1,0:T(8,128)}, f32[512,128]{1,0:T(8,128)}, f32[128,512]{1,0:T(8,128)}, ...) | async-done | bytes 1048592 | tf_op jit(solution)/shard_map/psum | solution.py:117
  329.8 15.8 %scatter_custom_fusion.1 = f32[8192,128]{1,0:T(8,128)} fusion(s32[2304]{0:T(1024)} %copy-done.14, f32[]{:T(128)} %constant.90.clone.1, bf16[2304,128]{1,0:T(8,128)(2,1)S(1)} %bitcast.32), kind=kCustom, calls=%fused_computation.17 | custom fusion | flops 589824 | bytes 4784640 | tf_op jit(solution)/shard_map/scatter-add | solution.py:112
  345.6 3.5 multiply_reduce_fusion
  349.7 4.2 %divide_subtract_fusion = f32[8192,128]{1,0:T(8,128)} fusion(f32[8192,128]{1,0:T(8,128)S(1)} %copy-done.1, f32[8192,128]{1,0:T(8,128)} %scatter_custom_fusion.1, f32[8192]{0:T(1024)S(1)} %get-tuple-element.25), kind=kLoop, calls=%fused_computation.9 | loop fusion | flops 3145728 | bytes 12615680 | tf_op jit(solution)/shard_map/sub | solution.py:115
  (106 shorter events, 32.9 us)
Async XLA Ops:
  7.2 84.7 %copy-start = (f32[512,128]{1,0:T(8,128)S(1)}, f32[512,128]{1,0:T(8,128)}, u32[]{:S(2)}) copy-start(f32[512,128]{1,0:T(8,128)} %param.15) | copy-start | bytes 786436
  53.1 4.7 %copy-start.16 = (s32[1,1536]{1,0:T(1,128)S(1)}, s32[1,1536]{1,0:T(1,128)}, u32[]{:S(2)}) copy-start(s32[1,1536]{1,0:T(1,128)} %param.17) | copy-start | bytes 18436
  54.2 32.9 %all-to-all-start.3 = ((f32[4,8,72,128]{3,2,0,1:T(8,128)}), f32[4,8,72,128]{3,2,0,1:T(8,128)S(1)}, u32[]{:S(2)}, u32[]{:S(2)}) async-start(f32[4,8,72,128]{3,2,0,1:T(8,128)} %copy.27), calls=%async_computation.3 | async-start | bytes 2359296 | tf_op jit(solution)/shard_map/all_to_all | solution.py:58
  57.8 63.4 %all-gather.3.cloned.1.call-start = ((), (), s32[]{:S(2)}) async-start(), calls=%async_computation.6 | async-start | bytes 1310720 | tf_op jit(solution)/shard_map/all_gather | solution.py:78
  87.2 2.9 copy-start.12
  91.9 52.7 %copy-start.4 = (f32[1024,512]{1,0:T(8,128)}, f32[1024,512]{1,0:T(8,128)S(1)}, u32[]{:S(2)}) copy-start(f32[1024,512]{1,0:T(8,128)S(1)} %fusion.30) | copy-start | bytes 6291460
  91.9 4.3 %copy-start.10 = (f32[128,512]{1,0:T(8,128)S(1)}, f32[128,512]{1,0:T(8,128)}, u32[]{:S(2)}) copy-start(f32[128,512]{1,0:T(8,128)} %param.12) | copy-start | bytes 786436
  94.7 5.3 %copy-start.19 = (f32[1024]{0:T(1024)}, f32[1024]{0:T(1024)S(1)}, u32[]{:S(2)}) copy-start(f32[1024]{0:T(1024)S(1)} %get-tuple-element.33) | copy-start | bytes 12292
  95.4 4.6 %copy-start.17 = (f32[1024]{0:T(1024)}, f32[1024]{0:T(1024)S(1)}, u32[]{:S(2)}) copy-start(f32[1024]{0:T(1024)S(1)} %get-tuple-element.28) | copy-start | bytes 12292
  97.2 2.7 copy-start.8
  97.2 3.4 copy-start.3
  100.0 12.9 %copy-start.20 = (f32[512]{0:T(512)}, f32[512]{0:T(512)S(1)}, u32[]{:S(2)}) copy-start(f32[512]{0:T(512)S(1)} %get-tuple-element.32) | copy-start | bytes 6148
  121.2 5.8 %copy-start.22 = (f32[512]{0:T(512)S(1)}, f32[512]{0:T(512)}, u32[]{:S(2)}) copy-start(f32[512]{0:T(512)} %get-tuple-element.23) | copy-start | bytes 6148
  142.3 10.8 %slice-start = ((s8[8388608]{0:T(1024)(128)(4,1)}), s8[4194304]{0:T(1024)(128)(4,1)S(1)}, s32[]{:S(2)}) async-start(s8[8388608]{0:T(1024)(128)(4,1)} %bitcast.28), calls=%async_computation.8 | async-start | bytes 8388608
  144.6 3.8 %copy-start.25 = (f32[1024]{0:T(1024)}, f32[1024]{0:T(1024)S(1)}, u32[]{:S(2)}) copy-start(f32[1024]{0:T(1024)S(1)} %multiply_multiply_fusion) | copy-start | bytes 12292
  144.6 8.5 %slice-start.1 = ((s8[8388608]{0:T(1024)(128)(4,1)}), s8[4194304]{0:T(1024)(128)(4,1)S(1)}, s32[]{:S(2)}) async-start(s8[8388608]{0:T(1024)(128)(4,1)} %bitcast.28), calls=%async_computation.9 | async-start | bytes 8388608
  154.8 2.6 copy-start.27
  160.0 13.7 %copy-start.18 = (f32[1024]{0:T(1024)S(1)}, f32[1024]{0:T(1024)}, u32[]{:S(2)}) copy-start(f32[1024]{0:T(1024)} %copy-done.17) | copy-start | bytes 12292
  160.0 13.7 %copy-start.26 = (f32[1024]{0:T(1024)S(1)}, f32[1024]{0:T(1024)}, u32[]{:S(2)}) copy-start(f32[1024]{0:T(1024)} %copy-done.25) | copy-start | bytes 12292
  170.2 10.4 %all-to-all-start.4 = ((bf16[4,8,72,128]{3,2,1,0:T(8,128)(2,1)}), bf16[4,8,72,128]{3,2,1,0:T(8,128)(2,1)S(1)}, u32[]{:S(2)}, u32[]{:S(2)}) async-start(bf16[4,8,72,128]{3,2,1,0:T(8,128)(2,1)} %bitcast.33), calls=%async_computation.4 | async-start | bytes 1179648 | tf_op jit(solution)/shard_map/all_to_all | solution.py:97
  181.5 148.2 %all-to-all-start.5 = ((bf16[4,8,72,128]{3,2,0,1:T(8,128)(2,1)}), bf16[4,8,72,128]{3,2,0,1:T(8,128)(2,1)S(1)}, u32[]{:S(2)}, u32[]{:S(2)}) async-start(bf16[4,8,72,128]{3,2,0,1:T(8,128)(2,1)} %copy.29), calls=%async_computation.5 | async-start | bytes 1179648 | tf_op jit(solution)/shard_map/all_to_all | solution.py:96
  186.1 139.9 %all-reduce.3.cloned.1.call-start = ((), (), s32[]{:S(2)}) async-start(), calls=%async_computation.7 | async-start | bytes 2097152 | tf_op jit(solution)/shard_map/psum | solution.py:117
  345.6 3.5 copy-start.15
  345.6 4.1 %copy-start.1 = (f32[8192,128]{1,0:T(8,128)S(1)}, f32[8192,128]{1,0:T(8,128)}, u32[]{:S(2)}) copy-start(f32[8192,128]{1,0:T(8,128)} %param.10) | copy-start | bytes 12582916
  (11 other events, 16.5 us)
Sparse Core Ops, SparseCore 0:
  96.4 24.8 all-gather.2
  193.0 132.9 all-reduce.2
where the time goes:
time: 363 us; the launch traced here: 362 us
  waiting for transfers between devices  135 us (37%)
  blocking collectives  99.8 us (27%)
  other arithmetic  45.6 us (13%)
  matrix products  41 us (11%)
  between operations  16.3 us (4%)
  local copies, waits for them, and re-layouts  12.4 us (3%)
  starting transfers between devices  11.7 us (3%)
    psum x1, waiting for transfers between devices, per_device(): lax.psum((user_first_g, user_second_g, item_first_g, item_second_g, loss_...  96.8 us
    psum x1, blocking collectives, per_device(): lax.psum((user_first_g, user_second_g, item_first_g, item_second_g, loss_...  40.8 us
    all_to_all x1, waiting for transfers between devices, per_device(): lax.all_to_all(lax.all_to_all(fetched, 'dp', split_axis=0, concat_axis=0,...  29.1 us
    dot_general x6, matrix products, tower_pass(): jnp.dot(hidden_act, second_w, precision=highest, preferred_element_type=j...  19.6 us
    all_to_all x1, blocking collectives, per_device(): lax.all_to_all(fetched, 'dp', split_axis=0, concat_axis=0, tiled=True)  18.2 us
    scatter-add x1, other arithmetic, per_device(): grad_rows = jnp.zeros_like(id_table).at[asked_rows.reshape(-1)].add(sent_...  15.8 us
    all_gather x1, blocking collectives, per_device(): lax.all_gather(user_vec, 'dp', axis=0, tiled=True).astype(jnp.bfloat16)  11.5 us
    all_to_all x1, blocking collectives, per_device(): lax.all_to_all(lax.all_to_all(fetch_rows[0], 'dp', split_axis=0, concat_a...  10.3 us
  transfers between devices with their start and end apart: 5, of which 4 were waited for; matrix products, arithmetic and copies ran while one was open for 4% of the time, Pallas kernels for 0%

commit v1 on v0

--- a/solution.py
+++ b/solution.py
@@ -55,12 +55,20 @@
     fetched = jnp.take(id_table, asked_rows.reshape(-1), axis=0).reshape(
         asked_rows.shape + (target_index_vector,)
     )
-    returned = lax.all_to_all(
-        lax.all_to_all(fetched, "dp", split_axis=0, concat_axis=0, tiled=True),
-        "shard",
-        split_axis=1,
-        concat_axis=1,
-        tiled=True,
+    returned = jnp.concatenate(
+        lax.all_to_all(
+            jnp.stack(
+                jnp.split(
+                    lax.all_to_all(fetched, "dp", split_axis=0, concat_axis=0, tiled=True),
+                    lax.axis_size("shard"),
+                    axis=1,
+                )
+            ),
+            "shard",
+            0,
+            0,
+        ),
+        axis=1,
     )
     slot_rows = returned.reshape(-1, target_index_vector)
     slot_index = lookup_slots[0]

time: 363 us -> 367 us (1.011)
  local copies, waits for them, and re-layouts: 12.4 us -> 16.6 us
    unnamed x60 -> x67, local copies, waits for them, and re-layouts: 1.49 us -> 6.19 us
where the time goes in v1:
time: 367 us; the launch traced here: 366 us
  waiting for transfers between devices  135 us (37%)
  blocking collectives  99.7 us (27%)
  other arithmetic  45.6 us (12%)
  matrix products  41 us (11%)
  local copies, waits for them, and re-layouts  16.6 us (5%)
  between operations  16.3 us (4%)
  starting transfers between devices  11.7 us (3%)
    psum x1, waiting for transfers between devices, per_device(): lax.psum((user_first_g, user_second_g, item_first_g, item_second_g, loss_...  96.8 us
    psum x1, blocking collectives, per_device(): lax.psum((user_first_g, user_second_g, item_first_g, item_second_g, loss_...  40.8 us
    all_to_all x1, waiting for transfers between devices, per_device(): lax.all_to_all(jnp.stack(jnp.split(lax.all_to_all(fetched, 'dp', split_ax...  29.1 us
    dot_general x6, matrix products, tower_pass(): jnp.dot(hidden_act, second_w, precision=highest, preferred_element_type=j...  19.6 us
    all_to_all x1, blocking collectives, per_device(): lax.all_to_all(fetched, 'dp', split_axis=0, concat_axis=0, tiled=True)  18.2 us
    scatter-add x1, other arithmetic, per_device(): grad_rows = jnp.zeros_like(id_table).at[asked_rows.reshape(-1)].add(sent_...  15.8 us
    all_gather x1, blocking collectives, per_device(): lax.all_gather(user_vec, 'dp', axis=0, tiled=True).astype(jnp.bfloat16)  11.5 us
    all_to_all x1, blocking collectives, per_device(): lax.all_to_all(lax.all_to_all(fetch_rows[0], 'dp', split_axis=0, concat_a...  10.3 us
  transfers between devices with their start and end apart: 5, of which 4 were waited for; matrix products, arithmetic and copies ran while one was open for 4% of the time, Pallas kernels for 0%

profile of v1, /device:TPU:0, one launch (start us, length us, event | category | flops | bytes accessed | tf_op | source)
XLA Modules:
  0.0 366.1 jit_solution(4604862800508863876)
XLA Ops:
  7.2 10.0 %all_to_all.30 = s32[4,8,72]{2,1,0:T(8,128)S(1)} all-to-all(s32[4,8,72]{2,1,0:T(8,128)} %bitcast.82), channel_id=1, replica_groups=mesh['dp'=4,'shard'=8] {'dp'}, dimensions={0} | all-to-all | bytes 18432 | tf_op jit(solution)/shard_map/all_to_all | solution.py:49
  17.2 10.3 %all_to_all.31 = s32[4,8,72]{2,0,1:T(4,128)S(1)} all-to-all(s32[4,8,72]{2,0,1:T(4,128)S(1)} %copy.54), channel_id=1, replica_groups=mesh['dp'=4,'shard'=8] {'shard'}, dimensions={1} | all-to-all | bytes 18432 | tf_op jit(solution)/shard_map/all_to_all | solution.py:48
  28.3 6.1 %gather_fusion = f32[2304,128]{1,0:T(8,128)S(1)} fusion(f32[8192,128]{1,0:T(8,128)} %param.10, s32[3072]{0:T(1024)S(1)} %pad_clamp_fusion), kind=kCustom, calls=%fused_computation | custom fusion | bytes 2368512 | tf_op jit(solution)/shard_map/jit(_take)/gather | solution.py:55
  34.9 18.2 %all_to_all.32 = f32[4,8,72,128]{3,2,1,0:T(8,128)S(1)} all-to-all(f32[4,8,72,128]{3,2,1,0:T(8,128)S(1)} %broadcast_select_fusion), channel_id=1, replica_groups=mesh['dp'=4,'shard'=8] {'dp'}, dimensions={0} | all-to-all | bytes 2359296 | tf_op jit(solution)/shard_map/all_to_all | solution.py:62
  58.5 3.6 all-to-all-start.3
  62.2 29.1 %all-to-all-done.3 = f32[8,4,1,72,128]{4,3,1,2,0:T(8,128)S(1)} async-done(((f32[8,4,1,72,128]{4,3,1,2,0:T(8,128)}), f32[8,4,1,72,128]{4,3,1,2,0:T(8,128)S(1)}, u32[]{:S(2)}, u32[]{:S(2)}) %all-to-all-start.3) | async-done | bytes 1179680 | tf_op jit(solution)/shard_map/all_to_all | solution.py:59
  96.2 2.7 multiply_reduce_fusion.2
  101.5 2.7 multiply_reduce_fusion.4
  105.6 11.5 %all_gather.10 = bf16[2048,128]{0,1:T(8,128)(2,1)} all-gather(bf16[512,128]{0,1:T(8,128)(2,1)S(1)} %get-tuple-element.24), channel_id=1, replica_groups=mesh['dp'=4,'shard'=8] {'dp'}, dimensions={0}, use_global_device_ids=true | all-gather | bytes 655360 | tf_op jit(solution)/shard_map/all_gather | solution.py:90
  117.1 8.4 %all-gather.3.cloned.1.call-done = bf16[4096,128]{0,1:T(8,128)(2,1)} async-done(((bf16[1024,128]{0,1:T(8,128)(2,1)}), bf16[4096,128]{0,1:T(8,128)(2,1)}) %all-gather.3.cloned.1.call-update) | async-done | bytes 1048592 | tf_op jit(solution)/shard_map/all_gather | solution.py:86
  125.5 5.8 %fusion = (f32[512]{0:T(512)S(1)}, f32[512,4096]{1,0:T(8,128)}) fusion(bf16[512,128]{0,1:T(8,128)(2,1)S(1)} %get-tuple-element.24, bf16[4096,128]{0,1:T(8,128)(2,1)} %all-gather.3.cloned.1.call-done), kind=kOutput, calls=%fused_computation.6 | convolution fusion | flops 541064704 | bytes 9570304 | tf_op jit(solution)/shard_map/dot_general | solution.py:23
  131.9 8.8 %all-gather = f32[4,1,512]{2,1,0:T(1,128)} all-gather(f32[1,1,512]{2,1,0:T(1,128)S(1)} %bitcast.84), channel_id=1, replica_groups=mesh['dp'=4,'shard'=8] {'dp'}, dimensions={0}, use_global_device_ids=true | all-gather | bytes 10240 | tf_op jit(solution)/shard_map/all_gather | solution.py:91
  140.7 4.1 %fusion.10 = f32[1024,128]{0,1:T(8,128)} fusion(bf16[1024,128]{0,1:T(8,128)(2,1)S(1)} %copy-done.3, f32[2048]{0:T(1024)} %bitcast.83, bf16[2048,128]{0,1:T(8,128)(2,1)} %all_gather.10), kind=kOutput, calls=%fused_computation.19 | convolution fusion | flops 1080033280 | bytes 1318912 | tf_op jit(solution)/shard_map/dot_general | solution.py:40
  148.8 3.8 %fusion.6 = f32[1024,512]{1,0:T(8,128)S(1)} fusion(f32[1024,512]{1,0:T(8,128)S(1)} %fusion.30, f32[512,128]{1,0:T(8,128)S(1)} %copy-done, f32[1024,128]{0,1:T(8,128)} %copy-done.5, f32[1024,128]{0,1:T(8,128)} %fusion.37, f32[1024]{0:T(1024)S(1)} %multiply_multiply_fusion, f32[1024]{0:T(1024)} %copy-done.17), kind=kOutput, calls=%fused_computation.14 | convolution fusion | flops 810680320 | bytes 5513216 | tf_op jit(solution)/shard_map/transpose(jvp())/dot_general | solution.py:17
  159.0 2.6 fusion.43
  164.2 9.3 %scatter_custom_fusion = f32[2304,128]{1,0:T(8,128)S(1)} fusion(s32[1536]{0:T(1024)S(1)} %fusion.56, f32[1024,128]{1,0:T(8,128)} %fusion.66, f32[]{:T(128)} %constant.111, f32[512,128]{1,0:T(8,128)S(1)} %fusion.65, f32[]{:T(128)} %constant.90.clone.1), kind=kCustom, calls=%fused_computation.28 | custom fusion | flops 393216 | bytes 1966088 | tf_op jit(solution)/shard_map/scatter-add | solution.py:103
  174.5 3.5 all-to-all-start.4
  178.0 6.2 %fusion.32 = f32[512,128]{1,0:T(8,128)} fusion(f32[1024,512]{1,0:T(8,128)} %copy-done.4, f32[1024,128]{0,1:T(8,128)} %copy-done.5, f32[1024,128]{0,1:T(8,128)} %fusion.37, f32[1024]{0:T(1024)S(1)} %copy-done.26, f32[1024]{0:T(1024)S(1)} %copy-done.18), kind=kOutput, calls=%fused_computation.45 | convolution fusion | flops 808058880 | bytes 3416064 | tf_op jit(solution)/shard_map/transpose(jvp())/dot_general | solution.py:17
  185.8 4.6 %all-to-all-start.5 = ((bf16[4,8,72,128]{3,2,0,1:T(8,128)(2,1)}), bf16[4,8,72,128]{3,2,0,1:T(8,128)(2,1)S(1)}, u32[]{:S(2)}, u32[]{:S(2)}) async-start(bf16[4,8,72,128]{3,2,0,1:T(8,128)(2,1)} %copy.65), calls=%async_computation.5 | async-start | bytes 1179648 | tf_op jit(solution)/shard_map/all_to_all | solution.py:104
  191.9 40.8 %psum.39 = f32[]{:T(128)} all-reduce(f32[]{:T(128)} %get-tuple-element.29), channel_id=1, replica_groups=mesh['dp'=4,'shard'=8] {'dp','shard'}, use_global_device_ids=true, to_apply=%region_14.15 | all-reduce | flops 1 | bytes 8 | tf_op jit(solution)/shard_map/psum | solution.py:125
  233.4 96.8 %all-reduce.3.cloned.1.call-done = (f32[128,512]{1,0:T(8,128)}, f32[512,128]{1,0:T(8,128)}, f32[128,512]{1,0:T(8,128)}, f32[512,128]{1,0:T(8,128)}) async-done(((f32[128,512]{1,0:T(8,128)}, f32[512,128]{1,0:T(8,128)}, f32[128,512]{1,0:T(8,128)}, f32[512,128]{1,0:T(8,128)}), (f32[128,512]{1,0:T(8,128)}, f32[512,128]{1,0:T(8,128)}, f32[128,512]{1,0:T(8,128)}, ...) | async-done | bytes 1048592 | tf_op jit(solution)/shard_map/psum | solution.py:125
  334.0 15.8 %scatter_custom_fusion.1 = f32[8192,128]{1,0:T(8,128)} fusion(s32[2304]{0:T(1024)} %copy-done.14, f32[]{:T(128)} %constant.90.clone.1, bf16[2304,128]{1,0:T(8,128)(2,1)S(1)} %bitcast.80), kind=kCustom, calls=%fused_computation.17 | custom fusion | flops 589824 | bytes 4784640 | tf_op jit(solution)/shard_map/scatter-add | solution.py:120
  349.8 3.5 multiply_reduce_fusion
  354.0 4.2 %divide_subtract_fusion = f32[8192,128]{1,0:T(8,128)} fusion(f32[8192,128]{1,0:T(8,128)S(1)} %copy-done.1, f32[8192,128]{1,0:T(8,128)} %scatter_custom_fusion.1, f32[8192]{0:T(1024)S(1)} %get-tuple-element.25), kind=kLoop, calls=%fused_computation.9 | loop fusion | flops 3145728 | bytes 12615680 | tf_op jit(solution)/shard_map/sub | solution.py:123
  (113 shorter events, 37.2 us)
Async XLA Ops:
  7.2 89.0 %copy-start = (f32[512,128]{1,0:T(8,128)S(1)}, f32[512,128]{1,0:T(8,128)}, u32[]{:S(2)}) copy-start(f32[512,128]{1,0:T(8,128)} %param.15) | copy-start | bytes 786436
  54.5 7.7 %copy-start.16 = (s32[1,1536]{1,0:T(1,128)S(1)}, s32[1,1536]{1,0:T(1,128)}, u32[]{:S(2)}) copy-start(s32[1,1536]{1,0:T(1,128)} %param.17) | copy-start | bytes 18436
  58.5 32.9 %all-to-all-start.3 = ((f32[8,4,1,72,128]{4,3,1,2,0:T(8,128)}), f32[8,4,1,72,128]{4,3,1,2,0:T(8,128)S(1)}, u32[]{:S(2)}, u32[]{:S(2)}) async-start(f32[8,4,1,72,128]{4,3,1,2,0:T(8,128)} %fusion.47), calls=%async_computation.3 | async-start | bytes 2359296 | tf_op jit(solution)/shard_map/all_to_all | solution.py:59
  62.1 63.4 %all-gather.3.cloned.1.call-start = ((), (), s32[]{:S(2)}) async-start(), calls=%async_computation.6 | async-start | bytes 1310720 | tf_op jit(solution)/shard_map/all_gather | solution.py:86
  91.4 2.9 copy-start.12
  96.2 52.7 %copy-start.4 = (f32[1024,512]{1,0:T(8,128)}, f32[1024,512]{1,0:T(8,128)S(1)}, u32[]{:S(2)}) copy-start(f32[1024,512]{1,0:T(8,128)S(1)} %fusion.30) | copy-start | bytes 6291460
  96.2 4.3 %copy-start.10 = (f32[128,512]{1,0:T(8,128)S(1)}, f32[128,512]{1,0:T(8,128)}, u32[]{:S(2)}) copy-start(f32[128,512]{1,0:T(8,128)} %param.12) | copy-start | bytes 786436
  98.9 5.3 %copy-start.19 = (f32[1024]{0:T(1024)}, f32[1024]{0:T(1024)S(1)}, u32[]{:S(2)}) copy-start(f32[1024]{0:T(1024)S(1)} %get-tuple-element.33) | copy-start | bytes 12292
  99.6 4.6 %copy-start.17 = (f32[1024]{0:T(1024)}, f32[1024]{0:T(1024)S(1)}, u32[]{:S(2)}) copy-start(f32[1024]{0:T(1024)S(1)} %get-tuple-element.28) | copy-start | bytes 12292
  101.5 2.7 copy-start.8
  101.5 3.4 copy-start.3
  104.3 12.9 %copy-start.20 = (f32[512]{0:T(512)}, f32[512]{0:T(512)S(1)}, u32[]{:S(2)}) copy-start(f32[512]{0:T(512)S(1)} %get-tuple-element.32) | copy-start | bytes 6148
  125.5 5.8 %copy-start.22 = (f32[512]{0:T(512)S(1)}, f32[512]{0:T(512)}, u32[]{:S(2)}) copy-start(f32[512]{0:T(512)} %get-tuple-element.23) | copy-start | bytes 6148
  146.5 10.8 %slice-start = ((s8[8388608]{0:T(1024)(128)(4,1)}), s8[4194304]{0:T(1024)(128)(4,1)S(1)}, s32[]{:S(2)}) async-start(s8[8388608]{0:T(1024)(128)(4,1)} %bitcast.75), calls=%async_computation.8 | async-start | bytes 8388608
  148.8 3.8 %copy-start.25 = (f32[1024]{0:T(1024)}, f32[1024]{0:T(1024)S(1)}, u32[]{:S(2)}) copy-start(f32[1024]{0:T(1024)S(1)} %multiply_multiply_fusion) | copy-start | bytes 12292
  148.8 8.5 %slice-start.1 = ((s8[8388608]{0:T(1024)(128)(4,1)}), s8[4194304]{0:T(1024)(128)(4,1)S(1)}, s32[]{:S(2)}) async-start(s8[8388608]{0:T(1024)(128)(4,1)} %bitcast.75), calls=%async_computation.9 | async-start | bytes 8388608
  159.0 2.6 copy-start.27
  164.2 13.7 %copy-start.18 = (f32[1024]{0:T(1024)S(1)}, f32[1024]{0:T(1024)}, u32[]{:S(2)}) copy-start(f32[1024]{0:T(1024)} %copy-done.17) | copy-start | bytes 12292
  164.2 13.7 %copy-start.26 = (f32[1024]{0:T(1024)S(1)}, f32[1024]{0:T(1024)}, u32[]{:S(2)}) copy-start(f32[1024]{0:T(1024)} %copy-done.25) | copy-start | bytes 12292
  174.5 10.4 %all-to-all-start.4 = ((bf16[4,8,72,128]{3,2,1,0:T(8,128)(2,1)}), bf16[4,8,72,128]{3,2,1,0:T(8,128)(2,1)S(1)}, u32[]{:S(2)}, u32[]{:S(2)}) async-start(bf16[4,8,72,128]{3,2,1,0:T(8,128)(2,1)} %bitcast.81), calls=%async_computation.4 | async-start | bytes 1179648 | tf_op jit(solution)/shard_map/all_to_all | solution.py:105
  185.8 148.2 %all-to-all-start.5 = ((bf16[4,8,72,128]{3,2,0,1:T(8,128)(2,1)}), bf16[4,8,72,128]{3,2,0,1:T(8,128)(2,1)S(1)}, u32[]{:S(2)}, u32[]{:S(2)}) async-start(bf16[4,8,72,128]{3,2,0,1:T(8,128)(2,1)} %copy.65), calls=%async_computation.5 | async-start | bytes 1179648 | tf_op jit(solution)/shard_map/all_to_all | solution.py:104
  190.4 139.9 %all-reduce.3.cloned.1.call-start = ((), (), s32[]{:S(2)}) async-start(), calls=%async_computation.7 | async-start | bytes 2097152 | tf_op jit(solution)/shard_map/psum | solution.py:125
  349.8 3.5 copy-start.15
  349.8 4.1 %copy-start.1 = (f32[8192,128]{1,0:T(8,128)S(1)}, f32[8192,128]{1,0:T(8,128)}, u32[]{:S(2)}) copy-start(f32[8192,128]{1,0:T(8,128)} %param.10) | copy-start | bytes 12582916
  (11 other events, 16.5 us)
Sparse Core Ops, SparseCore 0:
  100.6 24.7 all-gather.2
  197.3 132.9 all-reduce.2
